TPU v7x, 32 devices: a whole 2x2x4 slice. The times are simulated.
32 devices in a mesh: member: 2 (over x), dom: 16 (over z, y, core).
Axes of the slice: x: 2, y: 2, z: 4, core: 2. Of those that a mesh axis runs over, the one named last changes fastest.
Arguments:
- atom_feat: bfloat16 [128, 4096], P('member', 'dom'), parts along dimension 0, may hold values from -6 to 6
- bond_feat: bfloat16 [128, 32768], P('member', 'dom'), parts along dimension 0, may hold values from -6 to 6
- angle_feat: bfloat16 [128, 32768], P('member', 'dom'), parts along dimension 0, may hold values from -6 to 6
- atom_cot: bfloat16 [128, 4096], P('member', 'dom'), parts along dimension 0, may hold values from -6 to 6
- bond_cot: bfloat16 [128, 32768], P('member', 'dom'), parts along dimension 0, may hold values from -6 to 6
- angle_weight: bfloat16 [256, 256], P('member'), parts along dimension 0, may hold values from -0.375 to 0.375
- bond_weight: bfloat16 [128, 64], P('member'), parts along dimension 0, may hold values from -0.75 to 0.75
- message_weight: bfloat16 [256, 192], P('member'), parts along dimension 0, may hold values from -0.4375 to 0.4375
- out_weight: bfloat16 [128, 64], P('member'), parts along dimension 0, may hold values from -0.75 to 0.75
- send_list: int32 [16, 128], P('dom'), may hold values from 0 to 255
- bond_src: int32 [32768], P('dom'), may hold values from 0 to 383
- bond_dst: int32 [32768], P('dom'), may hold values from 0 to 383
- bond_count: int32 [16], replicated, may hold values from 1 to 2048, 13107 in all
- angle_first: int32 [32768], P('dom'), may hold values from 0 to 2047
- angle_second: int32 [32768], P('dom'), may hold values from 0 to 2047
- angle_count: int32 [16], replicated, may hold values from 1 to 2048, 13107 in all
Outputs:
- new_atom: bfloat16 [128, 4096], P('member', 'dom'), parts along dimension 0
- new_bond: bfloat16 [128, 32768], P('member', 'dom'), parts along dimension 0
- grad_atom: bfloat16 [128, 4096], P('member', 'dom'), parts along dimension 0
- grad_bond: bfloat16 [128, 32768], P('member', 'dom'), parts along dimension 0
There are 2 independent parts, one for each index of `member`. A program takes and returns all parts, laid end to end along the dimension named above; an argument that names none is the same for every part. Nothing has to cross between parts.
Inputs may be any that keep to these rules, and one draw needn't show every extreme that they name: `send_list`: indices into the listing partition's own atoms. `bond_src`: rows below 256 are the partition's own atoms, the others listed rows of partitions. `bond_dst`: same row space as bond_src. `bond_count`: live slots come first in each partition. `angle_count`: live slots come first in each partition.
All inputs are finite; a program needn't handle non-finite values.
Results may differ from a plain program's by a relative error of at most 0.0065.
Values may be sent and summed in bfloat16 or wider, within the bound.
A program may use at most 64 MiB of HBM per device.

v0:
```python
import functools

import jax
import jax.numpy as jnp
from jax import lax
from jax.experimental import pallas as pl
from jax.experimental.pallas import tpu as pltpu
from jax.sharding import PartitionSpec as P

F32 = jnp.float32
BF16 = jnp.bfloat16
GROUP = 256
CHUNK = 512


def dot(a, b):
    return lax.dot_general(a, b, (((1,), (0,)), ((), ())), preferred_element_type=F32)


def dot_nt(a, b):
    return lax.dot_general(a, b, (((1,), (1,)), ((), ())), preferred_element_type=F32)


def flip(a):
    return jnp.transpose(a.astype(F32)).astype(BF16)


def onehot(rows, index):
    grid = lax.broadcasted_iota(jnp.int32, (rows, index.shape[1]), 0)
    return jnp.where(grid == index, 1.0, 0.0).astype(BF16)


def wide_row(index, rows=16):
    return jnp.broadcast_to(index, (rows, index.shape[1])).astype(F32).astype(BF16)


def fill_table(table, index, cols):
    rows = table.shape[0]
    step = lax.broadcasted_iota(jnp.int32, (16, CHUNK), 0).astype(F32).astype(BF16)
    one = jnp.ones((16, CHUNK), BF16)
    zero = jnp.zeros((16, CHUNK), BF16)
    for base in range(0, rows, GROUP):
        wide = wide_row(index - base)
        for at in range(0, min(GROUP, rows - base), 16):
            table[base + at : base + at + 16, cols] = jnp.where(wide == step + at, one, zero)


def gate_parts(value):
    half = value.shape[0] // 2
    first = value[:half]
    sig_a = 0.5 * jnp.tanh(0.5 * first) + 0.5
    sig_c = 0.5 * jnp.tanh(0.5 * value[half:]) + 0.5
    prod = first * sig_a
    out = prod * sig_c
    return out, sig_c * (sig_a + prod * (1.0 - sig_a)), out * (1.0 - sig_c)


def pick_group(stacked, group, groups, width):
    acc = jnp.zeros((width, stacked.shape[1]), F32)
    group = jnp.broadcast_to(group, acc.shape)
    for k in range(groups):
        acc = jnp.where(group == k, stacked[k * width : (k + 1) * width], acc)
    return acc


INPUTS = 16


def kernel(n, axis, *refs):
    sources = refs[:INPUTS]
    outs = refs[INPUTS : INPUTS + 4]
    staged = refs[INPUTS + 4 : 2 * INPUTS + 4]
    in_sem = refs[2 * INPUTS + 4]
    copies = [
        pltpu.make_async_copy(sources[k], staged[k], in_sem.at[k]) for k in range(INPUTS)
    ]
    body(n, axis, copies, *staged, *outs, *refs[2 * INPUTS + 5 :])


def body(
    n,
    axis,
    copies,
    atom_ref,
    bond_ref,
    angle_ref,
    acot_ref,
    bcot_ref,
    wa_ref,
    wb_ref,
    wm_ref,
    wo_ref,
    list_ref,
    src_ref,
    dst_ref,
    first_ref,
    second_ref,
    bcount_ref,
    acount_ref,
    new_atom_ref,
    new_bond_ref,
    grad_atom_ref,
    grad_bond_ref,
    send_ref,
    recv_ref,
    send2_ref,
    recv2_ref,
    table_first,
    table_second,
    table_src,
    table_dst,
    stack_ref,
    z_ref,
    fac_ref,
    spread_ref,
    spread1_ref,
    spread2_ref,
    dst_rows_ref,
    dstval_ref,
    dtotal_ref,
    gsrc_ref,
    summed_ref,
    back_ref,
    dsum_ref,
    send_sem,
    recv_sem,
    send_sem2,
    recv_sem2,
):
    me = lax.axis_index(axis)
    width, atoms = atom_ref.shape
    bonds = bond_ref.shape[1]
    angles = angle_ref.shape[1]
    groups = bonds // GROUP
    slots = list_ref.shape[1]
    space_cols = atoms + slots

    barrier = pltpu.get_barrier_semaphore()

    def greet(turn, carry):
        pl.semaphore_signal(
            barrier,
            inc=1,
            device_id={axis: lax.rem(me + turn, n)},
            device_id_type=pl.DeviceIdType.MESH,
        )
        return carry

    for k in (0, 3, 8, 9, 12, 13, 10, 11, 14, 15, 1, 2, 5, 4, 6, 7):
        copies[k].start()
    lax.fori_loop(1, n, greet, 0)

    def ready(*which):
        for k in which:
            copies[k].wait()

    def count_of(ref):
        hit = lax.broadcasted_iota(jnp.int32, ref.shape, 1) == me
        return jnp.sum(jnp.where(hit, ref[...].astype(F32), 0.0), axis=1, keepdims=True).astype(
            jnp.int32
        )


    def copy_to(source, target, sems, rsems, turn):
        there = lax.rem(me + turn, n)
        return pltpu.make_async_remote_copy(
            src_ref=source.at[there],
            dst_ref=target.at[me],
            send_sem=sems.at[turn],
            recv_sem=rsems.at[turn],
            device_id={axis: there},
            device_id_type=pl.DeviceIdType.MESH,
        )

    def start_all(source, target, sems, rsems):
        def one(turn, carry):
            copy_to(source, target, sems, rsems, turn).start()
            return carry

        lax.fori_loop(1, n, one, 0)

    def wait_all(source, target, sems, rsems):
        def one(turn, carry):
            copy_to(source, target, sems, rsems, turn).wait()
            return carry

        lax.fori_loop(1, n, one, 0)

    ready(0, 3, 8, 9)
    wo_t = flip(wo_ref[...])
    atom_back = dot(wo_t, acot_ref[...]).astype(BF16)
    own = jnp.concatenate([atom_ref[...], atom_back], 0)
    table_list = onehot(atoms, list_ref[...])
    listed = dot(own, table_list)
    send_ref[...] = jnp.transpose(listed).reshape(send_ref.shape).astype(BF16)

    ready(12, 13)
    chunks = angles // CHUNK

    def angle_tables(turn, carry):
        cols = pl.ds(pl.multiple_of(turn * CHUNK, CHUNK), CHUNK)
        fill_table(table_second, second_ref[:, cols] & (GROUP - 1), cols)
        fill_table(table_first, first_ref[:, cols] & (GROUP - 1), cols)
        return carry

    lax.fori_loop(0, chunks, angle_tables, 0)
    pl.semaphore_wait(barrier, n - 1)
    start_all(send_ref, recv_ref, send_sem, recv_sem)
    recv_ref[me] = send_ref[me]

    ready(10, 11, 14, 15)
    bond_count = count_of(bcount_ref)
    angle_count = count_of(acount_ref)

    def bond_tables(turn, carry):
        cols = pl.ds(pl.multiple_of(turn * CHUNK, CHUNK), CHUNK)
        live = lax.broadcasted_iota(jnp.int32, (1, CHUNK), 1) + turn * CHUNK < bond_count
        fill_table(table_src, src_ref[:, cols], cols)
        fill_table(table_dst, jnp.where(live, dst_ref[:, cols], -1), cols)
        return carry

    lax.fori_loop(0, bonds // CHUNK, bond_tables, 0)

    ready(1, 2, 5)
    wa = wa_ref[...]
    for k in range(groups):
        stack_ref[k, width:, :] = bond_ref[:, k * GROUP : (k + 1) * GROUP]

    bond_stack = jnp.concatenate([stack_ref[k, width:, :] for k in range(groups)], 0)

    def second_step(turn, carry):
        cols = pl.ds(pl.multiple_of(turn * CHUNK, CHUNK), CHUNK)
        group = second_ref[:, cols] // GROUP
        got = pick_group(dot(bond_stack, table_second[:, cols]), group, groups, width)
        both = jnp.concatenate([got.astype(BF16), angle_ref[:, cols]], 0)
        z_ref[:, cols] = dot(wa[:, 2 * width :], both)
        return carry

    lax.fori_loop(0, chunks, second_step, 0)

    wait_all(send_ref, recv_ref, send_sem, recv_sem)
    received = jnp.transpose(recv_ref[...].astype(F32).reshape(slots, 2 * width)).astype(BF16)
    space = jnp.concatenate([own, received], 1)
    for k in range(groups):
        cols = slice(k * GROUP, (k + 1) * GROUP)
        stack_ref[k, :width, :] = dot(space[:width], table_src[:, cols]).astype(BF16)
        dst_rows_ref[:, cols] = dot(space, table_dst[:, cols])

    def first_group(turn, cols):
        at = lax.broadcasted_iota(jnp.int32, (1, CHUNK), 1) + turn * CHUNK
        return jnp.where(at < angle_count, first_ref[:, cols] // GROUP, -1)

    def expand(value, group, out, cols, span):
        wide = wide_row(group)
        one = jnp.ones((16, CHUNK), BF16)
        zero = jnp.zeros((16, CHUNK), BF16)
        value = value.reshape(span // 16, 16, CHUNK)
        for k in range(groups):
            mask = jnp.where(wide == jnp.full((16, CHUNK), k, BF16), one, zero)
            out[k * span : (k + 1) * span, cols] = (value * mask[None]).reshape(span, CHUNK)

    both_stack = stack_ref[...].reshape(groups * 2 * width, GROUP)

    def first_step(turn, carry):
        cols = pl.ds(pl.multiple_of(turn * CHUNK, CHUNK), CHUNK)
        group = first_group(turn, cols)
        got = pick_group(dot(both_stack, table_first[:, cols]), group, groups, 2 * width)
        z_val = z_ref[:, cols] + dot(wa[:, : 2 * width], got.astype(BF16))
        out, fac_a, fac_c = gate_parts(z_val)
        fac_ref[:width, cols] = fac_a
        fac_ref[width:, cols] = fac_c
        expand(out.astype(BF16), group, spread_ref, cols, width)
        return carry

    lax.fori_loop(0, chunks, first_step, 0)
    summed_ref[...] = dot_nt(spread_ref[...], table_first[...]).astype(BF16).reshape(summed_ref.shape)

    ready(4, 6, 7)
    wb = wb_ref[...]
    wb_t = flip(wb)
    wm_t = wm_ref[...]
    wm = flip(wm_t)

    join = 2 if groups % 2 == 0 else 1
    span = join * GROUP

    def bond_step(turn, carry):
        cols = pl.ds(pl.multiple_of(turn * span, span), span)
        at = [turn * join + k for k in range(join)]
        live = lax.broadcasted_iota(jnp.int32, (1, span), 1) + turn * span < bond_count
        summed = jnp.concatenate([summed_ref[k] for k in at], 1)
        source = jnp.concatenate([stack_ref[k, :width, :] for k in at], 1)
        update = jnp.where(live, dot(wb, summed), 0.0)
        new_bond = (bond_ref[:, cols].astype(F32) + update).astype(BF16)
        new_bond_ref[:, cols] = new_bond
        rows = dst_rows_ref[:, cols]
        hidden = dot(wm, jnp.concatenate([source, rows[:width].astype(BF16), new_bond], 0))
        out, fac_a, fac_c = gate_parts(hidden)
        up = rows[width:]
        dhidden = jnp.concatenate([up * fac_a, up * fac_c], 0).astype(BF16)
        back = dot(wm_t, dhidden)
        dtotal = bcot_ref[:, cols].astype(F32) + back[2 * width :]
        dtotal_ref[:, cols] = dtotal
        dsum = dot(wb_t, jnp.where(live, dtotal, 0.0).astype(BF16)).astype(BF16)
        for k in range(join):
            dsum_ref[at[k]] = dsum[:, k * GROUP : (k + 1) * GROUP]
        gsrc_ref[:, cols] = back[:width]
        dstval_ref[:width, cols] = out.astype(BF16)
        dstval_ref[width:, cols] = back[width : 2 * width].astype(BF16)
        return carry

    lax.fori_loop(0, groups // join, bond_step, 0)

    wa_t = flip(wa[:, : 3 * width])
    dsum_stack = dsum_ref[...].reshape(groups * width, GROUP)

    def back_step(turn, carry):
        cols = pl.ds(pl.multiple_of(turn * CHUNK, CHUNK), CHUNK)
        group = first_group(turn, cols)
        up = pick_group(dot(dsum_stack, table_first[:, cols]), group, groups, width)
        fac = fac_ref[:, cols]
        dz = jnp.concatenate([up * fac[:width], up * fac[width:]], 0).astype(BF16)
        back = dot(wa_t, dz).astype(BF16)
        back_ref[:, cols] = back[width:]
        expand(back[:width], group, spread_ref, cols, width)
        return carry

    lax.fori_loop(0, chunks, back_step, 0)
    back0 = dot_nt(spread_ref[...], table_first[...])
    gsrc = jnp.concatenate(
        [
            (gsrc_ref[:, k * GROUP : (k + 1) * GROUP] + back0[k * width : (k + 1) * width]).astype(BF16)
            for k in range(groups)
        ],
        1,
    )
    to_src = dot_nt(gsrc, table_src[...])
    to_dst = dot_nt(dstval_ref[...], table_dst[...])
    terms = jnp.concatenate([to_dst[:width], to_dst[width:] + to_src], 0)
    send2_ref[...] = jnp.transpose(terms[:, atoms:]).reshape(send2_ref.shape).astype(BF16)

    start_all(send2_ref, recv2_ref, send_sem2, recv_sem2)
    recv2_ref[me] = send2_ref[me]
    def late_step(turn, carry):
        cols = pl.ds(pl.multiple_of(turn * CHUNK, CHUNK), CHUNK)
        expand(back_ref[:width, cols], first_group(turn, cols), spread1_ref, cols, width)
        expand(back_ref[width:, cols], second_ref[:, cols] // GROUP, spread2_ref, cols, width)
        return carry

    lax.fori_loop(0, chunks, late_step, 0)
    back1 = dot_nt(spread1_ref[...], table_first[...])
    back2 = dot_nt(spread2_ref[...], table_second[...])
    for k in range(groups):
        cols = slice(k * GROUP, (k + 1) * GROUP)
        rows = slice(k * width, (k + 1) * width)
        grad_bond_ref[:, cols] = (dtotal_ref[:, cols] + back1[rows] + back2[rows]).astype(BF16)

    wait_all(send2_ref, recv2_ref, send_sem2, recv_sem2)
    returned = jnp.transpose(recv2_ref[...].astype(F32).reshape(slots, 2 * width)).astype(BF16)
    total = terms[:, :atoms] + dot_nt(returned, table_list)
    new_atom_ref[...] = (
        atom_ref[...].astype(F32) + dot(wo_ref[...], total[:width].astype(BF16))
    ).astype(BF16)
    grad_atom_ref[...] = (acot_ref[...].astype(F32) + total[width:]).astype(BF16)


def local(n, *args):
    (atom_feat, bond_feat, angle_feat) = args[:3]
    width, atoms = atom_feat.shape
    bonds = bond_feat.shape[1]
    angles = angle_feat.shape[1]
    slots = args[9].shape[1]
    groups = bonds // GROUP
    space_cols = atoms + slots
    args = list(args)
    for at in (10, 11, 13, 14):
        args[at] = args[at].reshape(1, -1)
    args[7] = args[7].T
    args = args[:12] + args[13:15] + [args[12].reshape(1, -1), args[15].reshape(1, -1)]
    vm = pl.BlockSpec(memory_space=pltpu.VMEM)
    anywhere = pl.BlockSpec(memory_space=pl.ANY)
    part = slots // n
    exchange = pltpu.VMEM((n, part, 2 * width), BF16)
    shapes = (atom_feat.shape, bond_feat.shape, atom_feat.shape, bond_feat.shape)
    held = pl.pallas_call(
        functools.partial(kernel, n, "dom"),
        out_shape=tuple(pltpu.VMEM(shape, BF16) for shape in shapes),
        in_specs=[anywhere] * INPUTS,
        out_specs=[vm] * 4,
        scratch_shapes=[pltpu.VMEM(arg.shape, arg.dtype) for arg in args]
        + [
            pltpu.SemaphoreType.DMA((INPUTS,)),
            exchange,
            exchange,
            exchange,
            exchange,
            pltpu.VMEM((GROUP, angles), BF16),
            pltpu.VMEM((GROUP, angles), BF16),
            pltpu.VMEM((space_cols, bonds), BF16),
            pltpu.VMEM((space_cols, bonds), BF16),
            pltpu.VMEM((groups, 2 * width, GROUP), BF16),
            pltpu.VMEM((2 * width, angles), F32),
            pltpu.VMEM((2 * width, angles), F32),
            pltpu.VMEM((groups * width, angles), BF16),
            pltpu.VMEM((groups * width, angles), BF16),
            pltpu.VMEM((groups * width, angles), BF16),
            pltpu.VMEM((2 * width, bonds), F32),
            pltpu.VMEM((2 * width, bonds), BF16),
            pltpu.VMEM((width, bonds), F32),
            pltpu.VMEM((width, bonds), F32),
            pltpu.VMEM((groups, width, GROUP), BF16),
            pltpu.VMEM((2 * width, angles), BF16),
            pltpu.VMEM((groups, width, GROUP), BF16),
            pltpu.SemaphoreType.DMA((n,)),
            pltpu.SemaphoreType.DMA((n,)),
            pltpu.SemaphoreType.DMA((n,)),
            pltpu.SemaphoreType.DMA((n,)),
        ],
        compiler_params=pltpu.CompilerParams(collective_id=0, has_side_effects=True),
    )(*args)
    return pl.pallas_call(
        write_out,
        out_shape=tuple(jax.ShapeDtypeStruct(shape, BF16) for shape in shapes),
        in_specs=[vm] * 4,
        out_specs=[pl.BlockSpec(memory_space=pl.ANY)] * 4,
        scratch_shapes=[pltpu.SemaphoreType.DMA((4,))],
    )(*(pltpu.with_memory_space_constraint(each, pltpu.VMEM) for each in held))


def write_out(*refs):
    sems = refs[8]
    copies = [pltpu.make_async_copy(refs[k], refs[4 + k], sems.at[k]) for k in range(4)]
    for copy in copies:
        copy.start()
    for copy in copies:
        copy.wait()


def solution(mesh):
    return jax.shard_map(
        functools.partial(local, mesh.shape["dom"]),
        mesh=mesh,
        in_specs=(
            P("member", "dom"),
            P("member", "dom"),
            P("member", "dom"),
            P("member", "dom"),
            P("member", "dom"),
            P("member", None),
            P("member", None),
            P("member", None),
            P("member", None),
            P("dom", None),
            P("dom"),
            P("dom"),
            P(),
            P("dom"),
            P("dom"),
            P(),
        ),
        out_specs=(P("member", "dom"), P("member", "dom"), P("member", "dom"), P("member", "dom")),
        check_vma=False,
    )
```

profile of v0, /device:TPU:0, one launch (start us, length us, event | category | flops | bytes accessed | tf_op | source)
XLA Modules:
  0.0 28.8 jit_solution(15041219705746680075)
XLA Ops:
  0.6 27.3 %shard_map.183 = (bf16[64,256]{1,0:T(8,128)(2,1)S(1)}, bf16[64,2048]{1,0:T(8,128)(2,1)S(1)}, bf16[64,256]{1,0:T(8,128)(2,1)S(1)}, bf16[64,2048]{1,0:T(8,128)(2,1)S(1)}) custom-call(bf16[64,256]{1,0:T(8,128)(2,1)} %refs_0_.1, bf16[64,2048]{1,0:T(8,128)(2,1)} %refs_1_.1, bf16[64,2048]{1,0:T(8,128)(2,1)} %refs_2_.1, bf16[64,256]{1,0:T(8,128)(2,1)} %refs_3_.1, ...), custom_call_target="tpu_custom_call" | custom-call | tf_op jit(solution)/shard_map/pallas_call | solution.py:385
  27.9 0.8 %shard_map.184 = (bf16[64,256]{1,0:T(8,128)(2,1)}, bf16[64,2048]{1,0:T(8,128)(2,1)}, bf16[64,256]{1,0:T(8,128)(2,1)}, bf16[64,2048]{1,0:T(8,128)(2,1)}) custom-call(bf16[64,256]{1,0:T(8,128)(2,1)S(1)} %get-tuple-element.8.refs_0_, bf16[64,2048]{1,0:T(8,128)(2,1)S(1)} %get-tuple-element.9.refs_1_, bf16[64,256]{1,0:T(8,128)(2,1)S(1)} %get-tuple-element.10.refs_2_, ...), custom_call_target="tpu_custom_call" | custom-call | tf_op jit(solution)/shard_map/pallas_call | solution.py:421
where the time goes:
time: 28.9 us; the launch traced here: 28.8 us
  Pallas kernels  28.1 us (97%)
  between operations  0.65 us (2%)
    pallas_call x1, Pallas kernels, local(): pl.pallas_call(functools.partial(kernel, n, 'dom'), out_shape=tuple((pltp...  27.3 us
    pallas_call x1, Pallas kernels, local(): pl.pallas_call(write_out, out_shape=tuple((jax.ShapeDtypeStruct(shape, BF...  0.85 us

commit v1 on v0

v1 whole, which is shorter than its diff:
```python
import functools

import jax
import jax.numpy as jnp
from jax import lax
from jax.experimental import pallas as pl
from jax.experimental.pallas import tpu as pltpu
from jax.sharding import PartitionSpec as P

F32 = jnp.float32
BF16 = jnp.bfloat16
GROUP = 256
CHUNK = 512


def dot(a, b):
    return lax.dot_general(a, b, (((1,), (0,)), ((), ())), preferred_element_type=F32)


def dot_nt(a, b):
    return lax.dot_general(a, b, (((1,), (1,)), ((), ())), preferred_element_type=F32)


def flip(a):
    return jnp.transpose(a.astype(F32)).astype(BF16)


def onehot(rows, index):
    grid = lax.broadcasted_iota(jnp.int32, (rows, index.shape[1]), 0)
    return jnp.where(grid == index, 1.0, 0.0).astype(BF16)


def wide_row(index, rows=16):
    return jnp.broadcast_to(index, (rows, index.shape[1])).astype(F32).astype(BF16)


def fill_table(table, index, cols):
    rows = table.shape[0]
    step = lax.broadcasted_iota(jnp.int32, (16, CHUNK), 0).astype(F32).astype(BF16)
    one = jnp.ones((16, CHUNK), BF16)
    zero = jnp.zeros((16, CHUNK), BF16)
    for base in range(0, rows, GROUP):
        wide = wide_row(index - base)
        for at in range(0, min(GROUP, rows - base), 16):
            table[base + at : base + at + 16, cols] = jnp.where(wide == step + at, one, zero)


def gate_parts(value):
    half = value.shape[0] // 2
    first = value[:half]
    sig_a = 0.5 * jnp.tanh(0.5 * first) + 0.5
    sig_c = 0.5 * jnp.tanh(0.5 * value[half:]) + 0.5
    prod = first * sig_a
    out = prod * sig_c
    return out, sig_c * (sig_a + prod * (1.0 - sig_a)), out * (1.0 - sig_c)


def pick_group(stacked, group, groups, width):
    acc = jnp.zeros((width, stacked.shape[1]), F32)
    group = jnp.broadcast_to(group, acc.shape)
    for k in range(groups):
        acc = jnp.where(group == k, stacked[k * width : (k + 1) * width], acc)
    return acc


def skewed(count, *stages):
    for turn in range(count + len(stages) - 1):
        for late in reversed(range(len(stages))):
            if 0 <= turn - late < count:
                stages[late](turn - late)


INPUTS = 16


def kernel(n, axis, *refs):
    sources = refs[:INPUTS]
    outs = refs[INPUTS : INPUTS + 4]
    staged = list(refs[INPUTS + 4 : 2 * INPUTS + 3])
    in_sem, zin_ref = refs[2 * INPUTS + 3 : 2 * INPUTS + 5]
    width = sources[0].shape[0]
    staged.insert(2, zin_ref.at[3 * width : 4 * width, :])
    copies = [
        pltpu.make_async_copy(sources[k], staged[k], in_sem.at[k]) for k in range(INPUTS)
    ]
    body(n, axis, copies, *staged, *outs, zin_ref, *refs[2 * INPUTS + 5 :])


def body(
    n,
    axis,
    copies,
    atom_ref,
    bond_ref,
    angle_ref,
    acot_ref,
    bcot_ref,
    wa_ref,
    wb_ref,
    wm_ref,
    wo_ref,
    list_ref,
    src_ref,
    dst_ref,
    first_ref,
    second_ref,
    bcount_ref,
    acount_ref,
    new_atom_ref,
    new_bond_ref,
    grad_atom_ref,
    grad_bond_ref,
    zin_ref,
    send_ref,
    recv_ref,
    send2_ref,
    recv2_ref,
    table_pair,
    table_source,
    table_dst,
    stack_ref,
    bin_ref,
    up_ref,
    fac_ref,
    spread_ref,
    summed_ref,
    dhid_ref,
    dtotal_ref,
    dlive_ref,
    dsum_ref,
    dz_ref,
    source_val,
    dst_val,
    back_ref,
    send_sem,
    recv_sem,
    send_sem2,
    recv_sem2,
):
    me = lax.axis_index(axis)
    width, atoms = atom_ref.shape
    bonds = bond_ref.shape[1]
    angles = first_ref.shape[1]
    groups = bonds // GROUP
    slots = list_ref.shape[1]
    bond_chunks = bonds // CHUNK
    angle_chunks = angles // CHUNK

    barrier = pltpu.get_barrier_semaphore()

    def greet(turn, carry):
        pl.semaphore_signal(
            barrier,
            inc=1,
            device_id={axis: lax.rem(me + turn, n)},
            device_id_type=pl.DeviceIdType.MESH,
        )
        return carry

    for k in (0, 3, 8, 9, 12, 13, 10, 11, 14, 15, 1, 2, 5, 4, 6, 7):
        copies[k].start()
    lax.fori_loop(1, n, greet, 0)

    def ready(*which):
        for k in which:
            copies[k].wait()

    def count_of(ref):
        hit = lax.broadcasted_iota(jnp.int32, ref.shape, 1) == me
        return jnp.sum(jnp.where(hit, ref[...].astype(F32), 0.0), axis=1, keepdims=True).astype(
            jnp.int32
        )

    def copy_to(source, target, sems, rsems, turn):
        there = lax.rem(me + turn, n)
        return pltpu.make_async_remote_copy(
            src_ref=source.at[there],
            dst_ref=target.at[me],
            send_sem=sems.at[turn],
            recv_sem=rsems.at[turn],
            device_id={axis: there},
            device_id_type=pl.DeviceIdType.MESH,
        )

    def start_all(source, target, sems, rsems):
        def one(turn, carry):
            copy_to(source, target, sems, rsems, turn).start()
            return carry

        lax.fori_loop(1, n, one, 0)

    def wait_all(source, target, sems, rsems):
        def one(turn, carry):
            copy_to(source, target, sems, rsems, turn).wait()
            return carry

        lax.fori_loop(1, n, one, 0)

    def at(chunk, base=0):
        return slice(base + chunk * CHUNK, base + (chunk + 1) * CHUNK)

    ready(0, 3, 8, 9)
    wo_t = flip(wo_ref[...])
    atom_back = dot(wo_t, acot_ref[...]).astype(BF16)
    own = jnp.concatenate([atom_ref[...], atom_back], 0)
    table_list = onehot(atoms, list_ref[...])
    listed = dot(own, table_list)
    send_ref[...] = jnp.transpose(listed).reshape(send_ref.shape).astype(BF16)
    own_atom = atom_ref[...]

    ready(12, 13)

    def angle_tables(turn, carry):
        cols = pl.ds(pl.multiple_of(turn * CHUNK, CHUNK), CHUNK)
        more = pl.ds(pl.multiple_of(angles + turn * CHUNK, CHUNK), CHUNK)
        fill_table(table_pair, first_ref[:, cols] & (GROUP - 1), cols)
        fill_table(table_pair, second_ref[:, cols] & (GROUP - 1), more)
        return carry

    lax.fori_loop(0, angle_chunks, angle_tables, 0)
    pl.semaphore_wait(barrier, n - 1)
    start_all(send_ref, recv_ref, send_sem, recv_sem)
    recv_ref[me] = send_ref[me]

    ready(10, 11, 14, 15)
    bond_count = count_of(bcount_ref)
    angle_count = count_of(acount_ref)

    def bond_tables(turn, carry):
        cols = pl.ds(pl.multiple_of(turn * CHUNK, CHUNK), CHUNK)
        live = lax.broadcasted_iota(jnp.int32, (1, CHUNK), 1) + turn * CHUNK < bond_count
        fill_table(table_source, src_ref[:, cols], cols)
        fill_table(table_dst, jnp.where(live, dst_ref[:, cols], -1), cols)
        return carry

    lax.fori_loop(0, bond_chunks, bond_tables, 0)

    ready(1, 2, 5)
    wa = wa_ref[...]
    wa_t = flip(wa[:, : 3 * width])
    for k in range(groups):
        stack_ref[k * width : (k + 1) * width, :] = bond_ref[:, k * GROUP : (k + 1) * GROUP]
    source = jnp.concatenate([src_ref[:, k * GROUP : (k + 1) * GROUP] for k in range(groups)], 0)
    stack_ref[groups * width :, :] = jnp.concatenate(
        [(source & (GROUP - 1)).astype(F32), (source // GROUP).astype(F32)], 0
    ).astype(BF16)

    def gather_first(chunk):
        group = first_ref[:, at(chunk)] // GROUP
        got = dot(stack_ref[...], table_pair[:, at(chunk)])
        zin_ref[width : 2 * width, at(chunk)] = pick_group(got, group, groups, width).astype(BF16)
        low = got[groups * width : groups * width + groups]
        high = got[groups * width + groups :]
        hit = lax.broadcasted_iota(jnp.int32, low.shape, 0) == group
        index = jnp.sum(jnp.where(hit, low + GROUP * high, 0.0), axis=0, keepdims=True)
        fill_table(table_source, index.astype(jnp.int32), at(chunk, bonds))

    def gather_second(chunk):
        group = second_ref[:, at(chunk)] // GROUP
        got = dot(stack_ref[: groups * width, :], table_pair[:, at(chunk, angles)])
        zin_ref[2 * width : 3 * width, at(chunk)] = pick_group(got, group, groups, width).astype(BF16)

    def own_angle(chunk):
        zin_ref[:width, at(chunk)] = dot(own_atom, table_source[:atoms, at(chunk, bonds)]).astype(BF16)

    def own_bond(chunk):
        bin_ref[:width, at(chunk)] = dot(own_atom, table_source[:atoms, at(chunk)]).astype(BF16)
        got = dot(own, table_dst[:atoms, at(chunk)]).astype(BF16)
        bin_ref[width : 2 * width, at(chunk)] = got[:width]
        up_ref[:, at(chunk)] = got[width:]

    for chunk in range(angle_chunks):
        gather_first(chunk)
    for chunk in range(angle_chunks):
        gather_second(chunk)
    for chunk in range(angle_chunks):
        own_angle(chunk)
    for chunk in range(bond_chunks):
        own_bond(chunk)

    ready(4, 6, 7)
    wb = wb_ref[...]
    wb_t = flip(wb)
    wm_t = wm_ref[...]
    wm = flip(wm_t)

    wait_all(send_ref, recv_ref, send_sem, recv_sem)
    received = jnp.transpose(recv_ref[...].astype(F32).reshape(slots, 2 * width)).astype(BF16)

    def first_group(chunk):
        place = lax.broadcasted_iota(jnp.int32, (1, CHUNK), 1) + chunk * CHUNK
        return jnp.where(place < angle_count, first_ref[:, at(chunk)] // GROUP, -1)

    def expand(value, group, cols):
        wide = wide_row(group)
        one = jnp.ones((16, CHUNK), BF16)
        zero = jnp.zeros((16, CHUNK), BF16)
        value = value.reshape(width // 16, 16, CHUNK)
        for k in range(groups):
            mask = jnp.where(wide == jnp.full((16, CHUNK), k, BF16), one, zero)
            spread_ref[k * width : (k + 1) * width, cols] = (value * mask[None]).reshape(width, CHUNK)

    def all_angle(chunk):
        got = dot(received[:width], table_source[atoms:, at(chunk, bonds)]).astype(BF16)
        zin_ref[:width, at(chunk)] = zin_ref[:width, at(chunk)] + got

    def all_bond(chunk):
        got = dot(received[:width], table_source[atoms:, at(chunk)]).astype(BF16)
        bin_ref[:width, at(chunk)] = bin_ref[:width, at(chunk)] + got
        got = dot(received, table_dst[atoms:, at(chunk)]).astype(BF16)
        bin_ref[width : 2 * width, at(chunk)] = bin_ref[width : 2 * width, at(chunk)] + got[:width]
        up_ref[:, at(chunk)] = up_ref[:, at(chunk)] + got[width:]

    def message(chunk):
        out, fac_a, fac_c = gate_parts(dot(wa, zin_ref[:, at(chunk)]))
        fac_ref[:width, at(chunk)] = fac_a.astype(BF16)
        fac_ref[width:, at(chunk)] = fac_c.astype(BF16)
        expand(out.astype(BF16), first_group(chunk), at(chunk))

    skewed(angle_chunks, all_angle, message)
    for chunk in range(bond_chunks):
        all_bond(chunk)
    summed = dot_nt(spread_ref[:, :angles], table_pair[:, :angles]).astype(BF16)
    for k in range(groups):
        summed_ref[:, k * GROUP : (k + 1) * GROUP] = summed[k * width : (k + 1) * width]


    def live_bond(chunk):
        return lax.broadcasted_iota(jnp.int32, (1, CHUNK), 1) + chunk * CHUNK < bond_count

    def update_bond(chunk):
        update = jnp.where(live_bond(chunk), dot(wb, summed_ref[:, at(chunk)]), 0.0)
        new_bond = (bond_ref[:, at(chunk)].astype(F32) + update).astype(BF16)
        new_bond_ref[:, at(chunk)] = new_bond
        bin_ref[2 * width :, at(chunk)] = new_bond

    def bond_message(chunk):
        out, fac_a, fac_c = gate_parts(dot(wm, bin_ref[:, at(chunk)]))
        up = up_ref[:, at(chunk)].astype(F32)
        dhid_ref[:width, at(chunk)] = (up * fac_a).astype(BF16)
        dhid_ref[width:, at(chunk)] = (up * fac_c).astype(BF16)
        dst_val[:width, at(chunk)] = out.astype(BF16)

    def bond_back(chunk):
        back = dot(wm_t, dhid_ref[:, at(chunk)])
        dtotal = bcot_ref[:, at(chunk)].astype(F32) + back[2 * width :]
        dtotal_ref[:, at(chunk)] = dtotal
        dlive_ref[:, at(chunk)] = jnp.where(live_bond(chunk), dtotal, 0.0).astype(BF16)
        source_val[:, at(chunk)] = back[:width].astype(BF16)
        dst_val[width:, at(chunk)] = back[width : 2 * width].astype(BF16)

    def summed_back(chunk):
        dsum = dot(wb_t, dlive_ref[:, at(chunk)]).astype(BF16)
        for k in range(CHUNK // GROUP):
            row = (chunk * (CHUNK // GROUP) + k) * width
            dsum_ref[row : row + width, :] = dsum[:, k * GROUP : (k + 1) * GROUP]

    skewed(bond_chunks, update_bond, bond_message, bond_back, summed_back)

    def angle_up(chunk):
        got = dot(dsum_ref[...], table_pair[:, at(chunk)])
        up = pick_group(got, first_group(chunk), groups, width).astype(BF16)
        dz_ref[:width, at(chunk)] = up * fac_ref[:width, at(chunk)]
        dz_ref[width:, at(chunk)] = up * fac_ref[width:, at(chunk)]

    def angle_back(chunk):
        back = dot(wa_t, dz_ref[:, at(chunk)]).astype(BF16)
        source_val[:, at(chunk, bonds)] = back[:width]
        back_ref[:, at(chunk)] = back[width:]

    skewed(angle_chunks, angle_up, angle_back)
    far_source = dot_nt(table_source[atoms:, :], source_val[...])
    far_dst = dot_nt(table_dst[atoms:, :], dst_val[...])
    far = jnp.concatenate([far_dst[:, :width], far_dst[:, width:] + far_source], 1)
    send2_ref[...] = far.reshape(send2_ref.shape).astype(BF16)

    start_all(send2_ref, recv2_ref, send_sem2, recv_sem2)
    recv2_ref[me] = send2_ref[me]

    def late(chunk):
        expand(back_ref[:width, at(chunk)], first_group(chunk), at(chunk))
        expand(back_ref[width:, at(chunk)], second_ref[:, at(chunk)] // GROUP, at(chunk, angles))

    near_source = dot_nt(table_source[:atoms, :], source_val[...])
    near_dst = dot_nt(table_dst[:atoms, :], dst_val[...])
    for chunk in range(angle_chunks):
        late(chunk)
    back = dot_nt(spread_ref[...], table_pair[...])
    for k in range(groups):
        cols = slice(k * GROUP, (k + 1) * GROUP)
        grad_bond_ref[:, cols] = (dtotal_ref[:, cols] + back[k * width : (k + 1) * width]).astype(BF16)

    wait_all(send2_ref, recv2_ref, send_sem2, recv_sem2)
    returned = dot(table_list, recv2_ref[...].reshape(slots, 2 * width))
    total = jnp.concatenate([near_dst[:, :width], near_dst[:, width:] + near_source], 1) + returned
    total = jnp.transpose(total)
    new_atom_ref[...] = (
        atom_ref[...].astype(F32) + dot(wo_ref[...], total[:width].astype(BF16))
    ).astype(BF16)
    grad_atom_ref[...] = (acot_ref[...].astype(F32) + total[width:]).astype(BF16)


def local(n, *args):
    (atom_feat, bond_feat, angle_feat) = args[:3]
    width, atoms = atom_feat.shape
    bonds = bond_feat.shape[1]
    angles = angle_feat.shape[1]
    slots = args[9].shape[1]
    groups = bonds // GROUP
    space_cols = atoms + slots
    args = list(args)
    for at in (10, 11, 13, 14):
        args[at] = args[at].reshape(1, -1)
    args[7] = args[7].T
    args = args[:12] + args[13:15] + [args[12].reshape(1, -1), args[15].reshape(1, -1)]
    vm = pl.BlockSpec(memory_space=pltpu.VMEM)
    anywhere = pl.BlockSpec(memory_space=pl.ANY)
    part = slots // n
    exchange = pltpu.VMEM((n, part, 2 * width), BF16)
    shapes = (atom_feat.shape, bond_feat.shape, atom_feat.shape, bond_feat.shape)
    held = pl.pallas_call(
        functools.partial(kernel, n, "dom"),
        out_shape=tuple(pltpu.VMEM(shape, BF16) for shape in shapes),
        in_specs=[anywhere] * INPUTS,
        out_specs=[vm] * 4,
        scratch_shapes=[
            pltpu.VMEM(arg.shape, arg.dtype) for k, arg in enumerate(args) if k != 2
        ]
        + [
            pltpu.SemaphoreType.DMA((INPUTS,)),
            pltpu.VMEM((4 * width, angles), BF16),
            exchange,
            exchange,
            exchange,
            exchange,
            pltpu.VMEM((GROUP, 2 * angles), BF16),
            pltpu.VMEM((space_cols, bonds + angles), BF16),
            pltpu.VMEM((space_cols, bonds), BF16),
            pltpu.VMEM((groups * width + 2 * groups, GROUP), BF16),
            pltpu.VMEM((3 * width, bonds), BF16),
            pltpu.VMEM((width, bonds), BF16),
            pltpu.VMEM((2 * width, angles), BF16),
            pltpu.VMEM((groups * width, 2 * angles), BF16),
            pltpu.VMEM((width, bonds), BF16),
            pltpu.VMEM((2 * width, bonds), BF16),
            pltpu.VMEM((width, bonds), F32),
            pltpu.VMEM((width, bonds), BF16),
            pltpu.VMEM((groups * width, GROUP), BF16),
            pltpu.VMEM((2 * width, angles), BF16),
            pltpu.VMEM((width, bonds + angles), BF16),
            pltpu.VMEM((2 * width, bonds), BF16),
            pltpu.VMEM((2 * width, angles), BF16),
            pltpu.SemaphoreType.DMA((n,)),
            pltpu.SemaphoreType.DMA((n,)),
            pltpu.SemaphoreType.DMA((n,)),
            pltpu.SemaphoreType.DMA((n,)),
        ],
        compiler_params=pltpu.CompilerParams(collective_id=0, has_side_effects=True),
    )(*args)
    return pl.pallas_call(
        write_out,
        out_shape=tuple(jax.ShapeDtypeStruct(shape, BF16) for shape in shapes),
        in_specs=[vm] * 4,
        out_specs=[pl.BlockSpec(memory_space=pl.ANY)] * 4,
        scratch_shapes=[pltpu.SemaphoreType.DMA((4,))],
    )(*(pltpu.with_memory_space_constraint(each, pltpu.VMEM) for each in held))


def write_out(*refs):
    sems = refs[8]
    copies = [pltpu.make_async_copy(refs[k], refs[4 + k], sems.at[k]) for k in range(4)]
    for copy in copies:
        copy.start()
    for copy in copies:
        copy.wait()


def solution(mesh):
    return jax.shard_map(
        functools.partial(local, mesh.shape["dom"]),
        mesh=mesh,
        in_specs=(
            P("member", "dom"),
            P("member", "dom"),
            P("member", "dom"),
            P("member", "dom"),
            P("member", "dom"),
            P("member", None),
            P("member", None),
            P("member", None),
            P("member", None),
            P("dom", None),
            P("dom"),
            P("dom"),
            P(),
            P("dom"),
            P("dom"),
            P(),
        ),
        out_specs=(P("member", "dom"), P("member", "dom"), P("member", "dom"), P("member", "dom")),
        check_vma=False,
    )
```

time: 28.9 us -> 22.8 us (0.79)
  Pallas kernels: 28.1 us -> 22 us
    pallas_call x1, Pallas kernels: 27.3 us -> 21.2 us  [local(): pl.pallas_call(functools.partial(kernel, n, 'dom'), out_shape=tuple((pltp...]
where the time goes in v1:
time: 22.8 us; the launch traced here: 22.7 us
  Pallas kernels  22 us (96%)
  between operations  0.65 us (3%)
    pallas_call x1, Pallas kernels, local(): pl.pallas_call(functools.partial(kernel, n, 'dom'), out_shape=tuple((pltp...  21.2 us
    pallas_call x1, Pallas kernels, local(): pl.pallas_call(write_out, out_shape=tuple((jax.ShapeDtypeStruct(shape, BF...  0.85 us

profile of v1, /device:TPU:0, one launch (start us, length us, event | category | flops | bytes accessed | tf_op | source)
XLA Modules:
  0.0 22.7 jit_solution(9790478814548339186)
XLA Ops:
  0.6 21.2 %shard_map.183 = (bf16[64,256]{1,0:T(8,128)(2,1)S(1)}, bf16[64,2048]{1,0:T(8,128)(2,1)S(1)}, bf16[64,256]{1,0:T(8,128)(2,1)S(1)}, bf16[64,2048]{1,0:T(8,128)(2,1)S(1)}) custom-call(bf16[64,256]{1,0:T(8,128)(2,1)} %refs_0_.1, bf16[64,2048]{1,0:T(8,128)(2,1)} %refs_1_.1, bf16[64,2048]{1,0:T(8,128)(2,1)} %refs_2_.1, bf16[64,256]{1,0:T(8,128)(2,1)} %refs_3_.1, ...), custom_call_target="tpu_custom_call" | custom-call | tf_op jit(solution)/shard_map/pallas_call | solution.py:421
  21.8 0.8 %shard_map.184 = (bf16[64,256]{1,0:T(8,128)(2,1)}, bf16[64,2048]{1,0:T(8,128)(2,1)}, bf16[64,256]{1,0:T(8,128)(2,1)}, bf16[64,2048]{1,0:T(8,128)(2,1)}) custom-call(bf16[64,256]{1,0:T(8,128)(2,1)S(1)} %get-tuple-element.8.refs_0_, bf16[64,2048]{1,0:T(8,128)(2,1)S(1)} %get-tuple-element.9.refs_1_, bf16[64,256]{1,0:T(8,128)(2,1)S(1)} %get-tuple-element.10.refs_2_, ...), custom_call_target="tpu_custom_call" | custom-call | tf_op jit(solution)/shard_map/pallas_call | solution.py:460

commit v2 on v1

--- a/solution.py
+++ b/solution.py
@@ -71,6 +71,12 @@
 
 
 INPUTS = 16
+PER_G = 2
+PER_O = 2
+PER_M = 2
+PER_B = 4
+PER_C = 2
+PER_L = 2
 
 
 def kernel(n, axis, *refs):
@@ -132,6 +138,7 @@
     source_val,
     dst_val,
     back_ref,
+    near_ref,
     send_sem,
     recv_sem,
     send_sem2,
@@ -176,8 +183,8 @@
         return pltpu.make_async_remote_copy(
             src_ref=source.at[there],
             dst_ref=target.at[me],
-            send_sem=sems.at[turn],
-            recv_sem=rsems.at[turn],
+            send_sem=sems,
+            recv_sem=rsems,
             device_id={axis: there},
             device_id_type=pl.DeviceIdType.MESH,
         )
@@ -190,14 +197,39 @@
         lax.fori_loop(1, n, one, 0)
 
     def wait_all(source, target, sems, rsems):
-        def one(turn, carry):
-            copy_to(source, target, sems, rsems, turn).wait()
+        pltpu.make_async_remote_copy(
+            src_ref=source.at[pl.ds(0, n - 1)],
+            dst_ref=target.at[pl.ds(0, n - 1)],
+            send_sem=sems,
+            recv_sem=rsems,
+            device_id={axis: lax.rem(me + 1, n)},
+            device_id_type=pl.DeviceIdType.MESH,
+        ).wait()
+
+    def at(chunk, base=0):
+        return pl.ds(pl.multiple_of(base + chunk * CHUNK, CHUNK), CHUNK)
+
+    once = 1 + jnp.minimum(me, 0)
+
+    def staged(count, per, *stages):
+        def turn_of(turn, carry):
+            skewed(per, *(lambda k, stage=stage: stage(turn * per + k) for stage in stages))
             return carry
 
-        lax.fori_loop(1, n, one, 0)
-
-    def at(chunk, base=0):
-        return slice(base + chunk * CHUNK, base + (chunk + 1) * CHUNK)
+        lax.fori_loop(0, count // per if count > per else once, turn_of, 0)
+
+    def region(work):
+        def turn_of(turn, carry):
+            work()
+            return carry
+
+        lax.fori_loop(0, once, turn_of, 0)
+
+    def scatter(value, table, low, high):
+        middle = (low + high) // 2
+        return dot_nt(value[:, low:middle], table[:, low:middle]) + dot_nt(
+            value[:, middle:high], table[:, middle:high]
+        )
 
     ready(0, 3, 8, 9)
     wo_t = flip(wo_ref[...])
@@ -269,14 +301,8 @@
         bin_ref[width : 2 * width, at(chunk)] = got[:width]
         up_ref[:, at(chunk)] = got[width:]
 
-    for chunk in range(angle_chunks):
-        gather_first(chunk)
-    for chunk in range(angle_chunks):
-        gather_second(chunk)
-    for chunk in range(angle_chunks):
-        own_angle(chunk)
-    for chunk in range(bond_chunks):
-        own_bond(chunk)
+    staged(angle_chunks, PER_G, gather_first, gather_second)
+    staged(angle_chunks, PER_O, own_angle, own_bond)
 
     ready(4, 6, 7)
     wb = wb_ref[...]
@@ -317,12 +343,15 @@
         fac_ref[width:, at(chunk)] = fac_c.astype(BF16)
         expand(out.astype(BF16), first_group(chunk), at(chunk))
 
-    skewed(angle_chunks, all_angle, message)
-    for chunk in range(bond_chunks):
-        all_bond(chunk)
-    summed = dot_nt(spread_ref[:, :angles], table_pair[:, :angles]).astype(BF16)
-    for k in range(groups):
-        summed_ref[:, k * GROUP : (k + 1) * GROUP] = summed[k * width : (k + 1) * width]
+    staged(angle_chunks, PER_M, all_angle, message)
+    staged(bond_chunks, PER_O, all_bond)
+
+    def sum_messages():
+        summed = scatter(spread_ref, table_pair, 0, angles).astype(BF16)
+        for k in range(groups):
+            summed_ref[:, k * GROUP : (k + 1) * GROUP] = summed[k * width : (k + 1) * width]
+
+    region(sum_messages)
 
 
     def live_bond(chunk):
@@ -352,10 +381,10 @@
     def summed_back(chunk):
         dsum = dot(wb_t, dlive_ref[:, at(chunk)]).astype(BF16)
         for k in range(CHUNK // GROUP):
-            row = (chunk * (CHUNK // GROUP) + k) * width
-            dsum_ref[row : row + width, :] = dsum[:, k * GROUP : (k + 1) * GROUP]
-
-    skewed(bond_chunks, update_bond, bond_message, bond_back, summed_back)
+            row = pl.multiple_of((chunk * (CHUNK // GROUP) + k) * width, width)
+            dsum_ref[pl.ds(row, width), :] = dsum[:, k * GROUP : (k + 1) * GROUP]
+
+    staged(bond_chunks, PER_B, update_bond, bond_message, bond_back, summed_back)
 
     def angle_up(chunk):
         got = dot(dsum_ref[...], table_pair[:, at(chunk)])
@@ -368,11 +397,24 @@
         source_val[:, at(chunk, bonds)] = back[:width]
         back_ref[:, at(chunk)] = back[width:]
 
-    skewed(angle_chunks, angle_up, angle_back)
-    far_source = dot_nt(table_source[atoms:, :], source_val[...])
-    far_dst = dot_nt(table_dst[atoms:, :], dst_val[...])
-    far = jnp.concatenate([far_dst[:, :width], far_dst[:, width:] + far_source], 1)
-    send2_ref[...] = far.reshape(send2_ref.shape).astype(BF16)
+    staged(angle_chunks, PER_C, angle_up, angle_back)
+
+    def pooled_rows(rows):
+        parts = [
+            dot_nt(table_source[rows, :bonds], source_val[:, :bonds]),
+            dot_nt(table_source[rows, bonds:], source_val[:, bonds:]),
+        ]
+        half = bonds // 2
+        both = dot_nt(table_dst[rows, :half], dst_val[:, :half]) + dot_nt(
+            table_dst[rows, half:], dst_val[:, half:]
+        )
+        return jnp.concatenate([both[:, :width], both[:, width:] + parts[0] + parts[1]], 1)
+
+    def far_rows():
+        far = pooled_rows(slice(atoms, atoms + slots))
+        send2_ref[...] = far.reshape(send2_ref.shape).astype(BF16)
+
+    region(far_rows)
 
     start_all(send2_ref, recv2_ref, send_sem2, recv_sem2)
     recv2_ref[me] = send2_ref[me]
@@ -381,19 +423,25 @@
         expand(back_ref[:width, at(chunk)], first_group(chunk), at(chunk))
         expand(back_ref[width:, at(chunk)], second_ref[:, at(chunk)] // GROUP, at(chunk, angles))
 
-    near_source = dot_nt(table_source[:atoms, :], source_val[...])
-    near_dst = dot_nt(table_dst[:atoms, :], dst_val[...])
-    for chunk in range(angle_chunks):
-        late(chunk)
-    back = dot_nt(spread_ref[...], table_pair[...])
-    for k in range(groups):
-        cols = slice(k * GROUP, (k + 1) * GROUP)
-        grad_bond_ref[:, cols] = (dtotal_ref[:, cols] + back[k * width : (k + 1) * width]).astype(BF16)
+    def near_rows():
+        near_ref[...] = pooled_rows(slice(0, atoms))
+
+    region(near_rows)
+    staged(angle_chunks, PER_L, late)
+
+    def bond_grads():
+        back = scatter(spread_ref, table_pair, 0, 2 * angles)
+        for k in range(groups):
+            cols = slice(k * GROUP, (k + 1) * GROUP)
+            grad_bond_ref[:, cols] = (
+                dtotal_ref[:, cols] + back[k * width : (k + 1) * width]
+            ).astype(BF16)
+
+    region(bond_grads)
 
     wait_all(send2_ref, recv2_ref, send_sem2, recv_sem2)
     returned = dot(table_list, recv2_ref[...].reshape(slots, 2 * width))
-    total = jnp.concatenate([near_dst[:, :width], near_dst[:, width:] + near_source], 1) + returned
-    total = jnp.transpose(total)
+    total = jnp.transpose(near_ref[...] + returned)
     new_atom_ref[...] = (
         atom_ref[...].astype(F32) + dot(wo_ref[...], total[:width].astype(BF16))
     ).astype(BF16)
@@ -450,10 +498,11 @@
             pltpu.VMEM((width, bonds + angles), BF16),
             pltpu.VMEM((2 * width, bonds), BF16),
             pltpu.VMEM((2 * width, angles), BF16),
-            pltpu.SemaphoreType.DMA((n,)),
-            pltpu.SemaphoreType.DMA((n,)),
-            pltpu.SemaphoreType.DMA((n,)),
-            pltpu.SemaphoreType.DMA((n,)),
+            pltpu.VMEM((atoms, 2 * width), F32),
+            pltpu.SemaphoreType.DMA,
+            pltpu.SemaphoreType.DMA,
+            pltpu.SemaphoreType.DMA,
+            pltpu.SemaphoreType.DMA,
         ],
         compiler_params=pltpu.CompilerParams(collective_id=0, has_side_effects=True),
     )(*args)

time: 22.8 us -> 23.2 us (1.018)
  Pallas kernels: 22 us -> 22.4 us
    pallas_call x1, Pallas kernels: 21.2 us -> 21.6 us  [local(): pl.pallas_call(functools.partial(kernel, n, 'dom'), out_shape=tuple((pltp...]
where the time goes in v2:
time: 23.2 us; the launch traced here: 23.1 us
  Pallas kernels  22.4 us (97%)
  between operations  0.65 us (3%)
    pallas_call x1, Pallas kernels, local(): pl.pallas_call(functools.partial(kernel, n, 'dom'), out_shape=tuple((pltp...  21.6 us
    pallas_call x1, Pallas kernels, local(): pl.pallas_call(write_out, out_shape=tuple((jax.ShapeDtypeStruct(shape, BF...  0.85 us

profile of v2, /device:TPU:0, one launch (start us, length us, event | category | flops | bytes accessed | tf_op | source)
XLA Modules:
  0.0 23.1 jit_solution(11889502401324734245)
XLA Ops:
  0.6 21.6 %shard_map.183 = (bf16[64,256]{1,0:T(8,128)(2,1)S(1)}, bf16[64,2048]{1,0:T(8,128)(2,1)S(1)}, bf16[64,256]{1,0:T(8,128)(2,1)S(1)}, bf16[64,2048]{1,0:T(8,128)(2,1)S(1)}) custom-call(bf16[64,256]{1,0:T(8,128)(2,1)} %refs_0_.1, bf16[64,2048]{1,0:T(8,128)(2,1)} %refs_1_.1, bf16[64,2048]{1,0:T(8,128)(2,1)} %refs_2_.1, bf16[64,256]{1,0:T(8,128)(2,1)} %refs_3_.1, ...), custom_call_target="tpu_custom_call" | custom-call | tf_op jit(solution)/shard_map/pallas_call | solution.py:469
  22.2 0.8 %shard_map.184 = (bf16[64,256]{1,0:T(8,128)(2,1)}, bf16[64,2048]{1,0:T(8,128)(2,1)}, bf16[64,256]{1,0:T(8,128)(2,1)}, bf16[64,2048]{1,0:T(8,128)(2,1)}) custom-call(bf16[64,256]{1,0:T(8,128)(2,1)S(1)} %get-tuple-element.8.refs_0_, bf16[64,2048]{1,0:T(8,128)(2,1)S(1)} %get-tuple-element.9.refs_1_, bf16[64,256]{1,0:T(8,128)(2,1)S(1)} %get-tuple-element.10.refs_2_, ...), custom_call_target="tpu_custom_call" | custom-call | tf_op jit(solution)/shard_map/pallas_call | solution.py:509

commit v3 on v2

--- a/solution.py
+++ b/solution.py
@@ -45,12 +45,13 @@
             table[base + at : base + at + 16, cols] = jnp.where(wide == step + at, one, zero)
 
 
-def gate_parts(value):
-    half = value.shape[0] // 2
-    first = value[:half]
-    sig_a = 0.5 * jnp.tanh(0.5 * first) + 0.5
-    sig_c = 0.5 * jnp.tanh(0.5 * value[half:]) + 0.5
-    prod = first * sig_a
+def gate_parts(halved):
+    half = halved.shape[0] // 2
+    first = halved[:half]
+    wide = 1.0 + jnp.tanh(first)
+    sig_a = 0.5 * wide
+    sig_c = 0.5 * jnp.tanh(halved[half:]) + 0.5
+    prod = first * wide
     out = prod * sig_c
     return out, sig_c * (sig_a + prod * (1.0 - sig_a)), out * (1.0 - sig_c)
 
@@ -71,25 +72,26 @@
 
 
 INPUTS = 16
+OUTPUTS = 6
 PER_G = 2
 PER_O = 2
 PER_M = 2
 PER_B = 4
-PER_C = 2
 PER_L = 2
 
 
 def kernel(n, axis, *refs):
     sources = refs[:INPUTS]
-    outs = refs[INPUTS : INPUTS + 4]
-    staged = list(refs[INPUTS + 4 : 2 * INPUTS + 3])
-    in_sem, zin_ref = refs[2 * INPUTS + 3 : 2 * INPUTS + 5]
+    outs = refs[INPUTS : INPUTS + OUTPUTS]
+    refs = refs[INPUTS + OUTPUTS :]
+    staged = list(refs[: INPUTS - 1])
+    in_sem, zin_ref = refs[INPUTS - 1 : INPUTS + 1]
     width = sources[0].shape[0]
     staged.insert(2, zin_ref.at[3 * width : 4 * width, :])
     copies = [
         pltpu.make_async_copy(sources[k], staged[k], in_sem.at[k]) for k in range(INPUTS)
     ]
-    body(n, axis, copies, *staged, *outs, zin_ref, *refs[2 * INPUTS + 5 :])
+    body(n, axis, copies, *staged, *outs, zin_ref, *refs[INPUTS + 1 :])
 
 
 def body(
@@ -112,10 +114,12 @@
     second_ref,
     bcount_ref,
     acount_ref,
-    new_atom_ref,
+    total_ref,
     new_bond_ref,
-    grad_atom_ref,
     grad_bond_ref,
+    kept_atom_ref,
+    kept_cot_ref,
+    kept_weight_ref,
     zin_ref,
     send_ref,
     recv_ref,
@@ -139,6 +143,7 @@
     dst_val,
     back_ref,
     near_ref,
+    z_ref,
     send_sem,
     recv_sem,
     send_sem2,
@@ -250,10 +255,6 @@
         return carry
 
     lax.fori_loop(0, angle_chunks, angle_tables, 0)
-    pl.semaphore_wait(barrier, n - 1)
-    start_all(send_ref, recv_ref, send_sem, recv_sem)
-    recv_ref[me] = send_ref[me]
-
     ready(10, 11, 14, 15)
     bond_count = count_of(bcount_ref)
     angle_count = count_of(acount_ref)
@@ -266,6 +267,10 @@
         return carry
 
     lax.fori_loop(0, bond_chunks, bond_tables, 0)
+
+    pl.semaphore_wait(barrier, n - 1)
+    start_all(send_ref, recv_ref, send_sem, recv_sem)
+    recv_ref[me] = send_ref[me]
 
     ready(1, 2, 5)
     wa = wa_ref[...]
@@ -292,8 +297,13 @@
         got = dot(stack_ref[: groups * width, :], table_pair[:, at(chunk, angles)])
         zin_ref[2 * width : 3 * width, at(chunk)] = pick_group(got, group, groups, width).astype(BF16)
 
+    wa_half = wa * 0.5
+
     def own_angle(chunk):
         zin_ref[:width, at(chunk)] = dot(own_atom, table_source[:atoms, at(chunk, bonds)]).astype(BF16)
+
+    def own_sum(chunk):
+        z_ref[:, at(chunk)] = dot(wa_half, zin_ref[:, at(chunk)])
 
     def own_bond(chunk):
         bin_ref[:width, at(chunk)] = dot(own_atom, table_source[:atoms, at(chunk)]).astype(BF16)
@@ -302,13 +312,13 @@
         up_ref[:, at(chunk)] = got[width:]
 
     staged(angle_chunks, PER_G, gather_first, gather_second)
-    staged(angle_chunks, PER_O, own_angle, own_bond)
+    staged(angle_chunks, PER_O, own_angle, own_bond, own_sum)
 
     ready(4, 6, 7)
     wb = wb_ref[...]
     wb_t = flip(wb)
     wm_t = wm_ref[...]
-    wm = flip(wm_t)
+    wm_half = flip(wm_t) * 0.5
 
     wait_all(send_ref, recv_ref, send_sem, recv_sem)
     received = jnp.transpose(recv_ref[...].astype(F32).reshape(slots, 2 * width)).astype(BF16)
@@ -326,10 +336,6 @@
             mask = jnp.where(wide == jnp.full((16, CHUNK), k, BF16), one, zero)
             spread_ref[k * width : (k + 1) * width, cols] = (value * mask[None]).reshape(width, CHUNK)
 
-    def all_angle(chunk):
-        got = dot(received[:width], table_source[atoms:, at(chunk, bonds)]).astype(BF16)
-        zin_ref[:width, at(chunk)] = zin_ref[:width, at(chunk)] + got
-
     def all_bond(chunk):
         got = dot(received[:width], table_source[atoms:, at(chunk)]).astype(BF16)
         bin_ref[:width, at(chunk)] = bin_ref[:width, at(chunk)] + got
@@ -337,14 +343,16 @@
         bin_ref[width : 2 * width, at(chunk)] = bin_ref[width : 2 * width, at(chunk)] + got[:width]
         up_ref[:, at(chunk)] = up_ref[:, at(chunk)] + got[width:]
 
+    reach = dot(wa_half[:, :width], received[:width]).astype(BF16)
+
     def message(chunk):
-        out, fac_a, fac_c = gate_parts(dot(wa, zin_ref[:, at(chunk)]))
+        z_half = z_ref[:, at(chunk)] + dot(reach, table_source[atoms:, at(chunk, bonds)])
+        out, fac_a, fac_c = gate_parts(z_half)
         fac_ref[:width, at(chunk)] = fac_a.astype(BF16)
         fac_ref[width:, at(chunk)] = fac_c.astype(BF16)
         expand(out.astype(BF16), first_group(chunk), at(chunk))
 
-    staged(angle_chunks, PER_M, all_angle, message)
-    staged(bond_chunks, PER_O, all_bond)
+    staged(angle_chunks, PER_M, message, all_bond)
 
     def sum_messages():
         summed = scatter(spread_ref, table_pair, 0, angles).astype(BF16)
@@ -364,7 +372,7 @@
         bin_ref[2 * width :, at(chunk)] = new_bond
 
     def bond_message(chunk):
-        out, fac_a, fac_c = gate_parts(dot(wm, bin_ref[:, at(chunk)]))
+        out, fac_a, fac_c = gate_parts(dot(wm_half, bin_ref[:, at(chunk)]))
         up = up_ref[:, at(chunk)].astype(F32)
         dhid_ref[:width, at(chunk)] = (up * fac_a).astype(BF16)
         dhid_ref[width:, at(chunk)] = (up * fac_c).astype(BF16)
@@ -393,11 +401,36 @@
         dz_ref[width:, at(chunk)] = up * fac_ref[width:, at(chunk)]
 
     def angle_back(chunk):
-        back = dot(wa_t, dz_ref[:, at(chunk)]).astype(BF16)
-        source_val[:, at(chunk, bonds)] = back[:width]
-        back_ref[:, at(chunk)] = back[width:]
-
-    staged(angle_chunks, PER_C, angle_up, angle_back)
+        back = dot(wa_t[:width], dz_ref[:, at(chunk)])
+        source_val[:, at(chunk, bonds)] = back.astype(BF16)
+
+    far_rows = slice(atoms, atoms + slots)
+
+    def back_and_far():
+        from_dst, from_source = [], []
+
+        def far_bond(chunk):
+            from_dst.append(dot_nt(table_dst[far_rows, at(chunk)], dst_val[:, at(chunk)]))
+            from_source.append(dot_nt(table_source[far_rows, at(chunk)], source_val[:, at(chunk)]))
+
+        def far_angle(chunk):
+            cols = at(chunk, bonds)
+            from_source.append(dot_nt(table_source[far_rows, cols], source_val[:, cols]))
+
+        def opening(chunk):
+            angle_up(chunk)
+            if chunk < bond_chunks:
+                far_bond(chunk)
+
+        skewed(angle_chunks, opening, angle_back, far_angle)
+        for chunk in range(angle_chunks, bond_chunks):
+            far_bond(chunk)
+        both = sum(from_dst[1:], from_dst[0])
+        single = sum(from_source[1:], from_source[0])
+        far = jnp.concatenate([both[:, :width], both[:, width:] + single], 1)
+        send2_ref[...] = far.reshape(send2_ref.shape).astype(BF16)
+
+    region(back_and_far)
 
     def pooled_rows(rows):
         parts = [
@@ -410,24 +443,24 @@
         )
         return jnp.concatenate([both[:, :width], both[:, width:] + parts[0] + parts[1]], 1)
 
-    def far_rows():
-        far = pooled_rows(slice(atoms, atoms + slots))
-        send2_ref[...] = far.reshape(send2_ref.shape).astype(BF16)
-
-    region(far_rows)
-
     start_all(send2_ref, recv2_ref, send_sem2, recv_sem2)
     recv2_ref[me] = send2_ref[me]
+
+    def late_back(chunk):
+        back_ref[:, at(chunk)] = dot(wa_t[width:], dz_ref[:, at(chunk)]).astype(BF16)
 
     def late(chunk):
         expand(back_ref[:width, at(chunk)], first_group(chunk), at(chunk))
         expand(back_ref[width:, at(chunk)], second_ref[:, at(chunk)] // GROUP, at(chunk, angles))
 
     def near_rows():
+        kept_atom_ref[...] = atom_ref[...]
+        kept_cot_ref[...] = acot_ref[...]
+        kept_weight_ref[...] = wo_ref[...]
         near_ref[...] = pooled_rows(slice(0, atoms))
 
     region(near_rows)
-    staged(angle_chunks, PER_L, late)
+    staged(angle_chunks, PER_L, late_back, late)
 
     def bond_grads():
         back = scatter(spread_ref, table_pair, 0, 2 * angles)
@@ -441,11 +474,7 @@
 
     wait_all(send2_ref, recv2_ref, send_sem2, recv_sem2)
     returned = dot(table_list, recv2_ref[...].reshape(slots, 2 * width))
-    total = jnp.transpose(near_ref[...] + returned)
-    new_atom_ref[...] = (
-        atom_ref[...].astype(F32) + dot(wo_ref[...], total[:width].astype(BF16))
-    ).astype(BF16)
-    grad_atom_ref[...] = (acot_ref[...].astype(F32) + total[width:]).astype(BF16)
+    total_ref[...] = near_ref[...] + returned
 
 
 def local(n, *args):
@@ -468,9 +497,16 @@
     shapes = (atom_feat.shape, bond_feat.shape, atom_feat.shape, bond_feat.shape)
     held = pl.pallas_call(
         functools.partial(kernel, n, "dom"),
-        out_shape=tuple(pltpu.VMEM(shape, BF16) for shape in shapes),
+        out_shape=(
+            pltpu.VMEM((atoms, 2 * width), F32),
+            pltpu.VMEM(bond_feat.shape, BF16),
+            pltpu.VMEM(bond_feat.shape, BF16),
+            pltpu.VMEM(atom_feat.shape, BF16),
+            pltpu.VMEM(atom_feat.shape, BF16),
+            pltpu.VMEM((width, width), BF16),
+        ),
         in_specs=[anywhere] * INPUTS,
-        out_specs=[vm] * 4,
+        out_specs=[vm] * OUTPUTS,
         scratch_shapes=[
             pltpu.VMEM(arg.shape, arg.dtype) for k, arg in enumerate(args) if k != 2
         ]
@@ -499,6 +535,7 @@
             pltpu.VMEM((2 * width, bonds), BF16),
             pltpu.VMEM((2 * width, angles), BF16),
             pltpu.VMEM((atoms, 2 * width), F32),
+            pltpu.VMEM((2 * width, angles), F32),
             pltpu.SemaphoreType.DMA,
             pltpu.SemaphoreType.DMA,
             pltpu.SemaphoreType.DMA,
@@ -509,17 +546,48 @@
     return pl.pallas_call(
         write_out,
         out_shape=tuple(jax.ShapeDtypeStruct(shape, BF16) for shape in shapes),
-        in_specs=[vm] * 4,
+        in_specs=[vm] * OUTPUTS,
         out_specs=[pl.BlockSpec(memory_space=pl.ANY)] * 4,
-        scratch_shapes=[pltpu.SemaphoreType.DMA((4,))],
+        scratch_shapes=[
+            pltpu.VMEM(atom_feat.shape, BF16),
+            pltpu.VMEM(atom_feat.shape, BF16),
+            pltpu.SemaphoreType.DMA((4,)),
+        ],
     )(*(pltpu.with_memory_space_constraint(each, pltpu.VMEM) for each in held))
 
 
-def write_out(*refs):
-    sems = refs[8]
-    copies = [pltpu.make_async_copy(refs[k], refs[4 + k], sems.at[k]) for k in range(4)]
-    for copy in copies:
-        copy.start()
+def write_out(
+    total_ref,
+    new_bond_ref,
+    grad_bond_ref,
+    atom_ref,
+    cot_ref,
+    weight_ref,
+    new_atom_out,
+    new_bond_out,
+    grad_atom_out,
+    grad_bond_out,
+    new_atom_ref,
+    grad_atom_ref,
+    sems,
+):
+    pairs = (
+        (new_bond_ref, new_bond_out),
+        (grad_bond_ref, grad_bond_out),
+        (grad_atom_ref, grad_atom_out),
+        (new_atom_ref, new_atom_out),
+    )
+    copies = [pltpu.make_async_copy(*pair, sems.at[k]) for k, pair in enumerate(pairs)]
+    width = atom_ref.shape[0]
+    copies[0].start()
+    copies[1].start()
+    total = jnp.transpose(total_ref[...])
+    grad_atom_ref[...] = (cot_ref[...].astype(F32) + total[width:]).astype(BF16)
+    copies[2].start()
+    new_atom_ref[...] = (
+        atom_ref[...].astype(F32) + dot(weight_ref[...], total[:width].astype(BF16))
+    ).astype(BF16)
+    copies[3].start()
     for copy in copies:
         copy.wait()
 

time: 23.2 us -> 21.6 us (0.931)
  Pallas kernels: 22.4 us -> 20.9 us
    pallas_call x1, Pallas kernels: 21.6 us -> 20 us  [local(): pl.pallas_call(functools.partial(kernel, n, 'dom'), out_shape=(pltpu.VMEM...]
where the time goes in v3:
time: 21.6 us; the launch traced here: 21.5 us
  Pallas kernels  20.9 us (97%)
  between operations  0.65 us (3%)
    pallas_call x1, Pallas kernels, local(): pl.pallas_call(functools.partial(kernel, n, 'dom'), out_shape=(pltpu.VMEM...  20 us
    pallas_call x1, Pallas kernels, local(): pl.pallas_call(write_out, out_shape=tuple((jax.ShapeDtypeStruct(shape, BF...  0.86 us

profile of v3, /device:TPU:0, one launch (start us, length us, event | category | flops | bytes accessed | tf_op | source)
XLA Modules:
  0.0 21.5 jit_solution(8023760463701509289)
XLA Ops:
  0.6 20.0 %shard_map.183 = (f32[256,128]{1,0:T(8,128)S(1)}, bf16[64,2048]{1,0:T(8,128)(2,1)S(1)}, bf16[64,2048]{1,0:T(8,128)(2,1)S(1)}, bf16[64,256]{1,0:T(8,128)(2,1)S(1)...) custom-call(bf16[64,256]{1,0:T(8,128)(2,1)} %refs_0_.1, bf16[64,2048]{1,0:T(8,128)(2,1)} %refs_1_.1, ...), custom_call_target="tpu_custom_call" | custom-call | tf_op jit(solution)/shard_map/pallas_call | solution.py:498
  20.6 0.9 %shard_map.184 = (bf16[64,256]{1,0:T(8,128)(2,1)}, bf16[64,2048]{1,0:T(8,128)(2,1)}, bf16[64,256]{1,0:T(8,128)(2,1)}, bf16[64,2048]{1,0:T(8,128)(2,1)}) custom-call(f32[256,128]{1,0:T(8,128)S(1)} %get-tuple-element.10.total_ref, bf16[64,2048]{1,0:T(8,128)(2,1)S(1)} %get-tuple-element.11.new_bond_ref, bf16[64,2048]{1,0:T(8,128)(2,1)S(1)} %get-tuple-element.12.grad_bond_ref, ...), custom_call_target="tpu_custom_call" | custom-call | tf_op jit(solution)/shard_map/pallas_call | solution.py:546
